TPU v7x, 32 devices: a whole 2x2x4 slice. The times are simulated.
32 devices in a mesh: ctx: 8 (over y, x, core), qry: 4 (over z).
Axes of the slice: x: 2, y: 2, z: 4, core: 2. Of those that a mesh axis runs over, the one named last changes fastest.
Arguments:
- idx_query: bfloat16 [32, 8192], P('ctx', 'qry'), may hold values from -200 to 200
- idx_weight: bfloat16 [32, 64], P('ctx', 'qry'), may hold values from -3 to 3
- idx_keys: bfloat16 [16384, 128], P('ctx'), may hold values from -6 to 6
- q_latent: bfloat16 [32, 73728], P(('ctx', 'qry')), may hold values from -400 to 400
- latent_cache: bfloat16 [16384, 576], P('ctx'), may hold values from -20 to 20
- page_ids: int32 [32, 32], P(('ctx', 'qry')), may hold values from 0 to 255, as said below
Outputs:
- index_logp: float32 [32, 16384], P(('ctx', 'qry'))
- latent_out: bfloat16 [32, 65536], P(('ctx', 'qry'))
Inputs may be any that keep to these rules, and one draw needn't show every extreme that they name: `page_ids`: each row names 32 distinct pages, and no page id appears twice in the 1 row of one device (aligned blocks of 1 row). Page p holds tokens p * 64 to p * 64 + 63; ctx index j holds pages j * 32 to (j + 1) * 32 - 1. Of the 32 ids in the rows of one device, at most 8 lie on one ctx index, and in every such block some ctx index holds exactly 8.
All inputs are finite; a program needn't handle non-finite values.
Results may differ from a plain program's by a relative error of at most 0.013.
Values may be sent and summed in bfloat16 or wider, within the bound.
A program may use at most 64 MiB of HBM per device.

v0:
```python
import jax
import jax.numpy as jnp
from jax import lax
from jax.sharding import PartitionSpec as P

H_IDX = 64
D_IDX = 128
H = 128
D_LAT = 512
D_ROPE = 64
QK_NOPE = 128
PAGE = 64
TOPP = 32


def slot_ranks(requests, pages_dev):
    owner_shard = requests // pages_dev
    positions = jnp.arange(requests.shape[-1])
    earlier = positions[None, :] < positions[:, None]
    same_owner = owner_shard[..., :, None] == owner_shard[..., None, :]
    slot_rank = jnp.sum((same_owner & earlier).astype(jnp.int32), axis=-1)
    return (owner_shard, slot_rank)


def per_device(idx_query, idx_weight, idx_keys, q_latent, latent_cache, page_ids):
    shard_count = lax.axis_size("ctx")
    group_count = lax.axis_size("qry")
    ctx_index = lax.axis_index("ctx")
    rows_dev = q_latent.shape[0]
    ctx_dev = idx_keys.shape[0]
    latent_width = latent_cache.shape[1]
    pages_dev = ctx_dev // PAGE
    capacity = max(2, 2 * rows_dev * TOPP // shard_count)
    group_size = shard_count * rows_dev
    local_query = idx_query.reshape(group_count, rows_dev, idx_query.shape[1])
    local_weight = idx_weight.reshape(group_count, rows_dev, idx_weight.shape[1])
    every_query, every_weight = (
        lax.all_gather(local_query, "ctx", axis=0, tiled=True),
        lax.all_gather(local_weight, "ctx", axis=0, tiled=True),
    )
    group_query, group_weight = (
        lax.all_to_all(
            every_query.reshape(shard_count, group_count, rows_dev, idx_query.shape[1]),
            "qry",
            split_axis=1,
            concat_axis=3,
            tiled=True,
        ),
        lax.all_to_all(
            every_weight.reshape(shard_count, group_count, rows_dev, idx_weight.shape[1]),
            "qry",
            split_axis=1,
            concat_axis=3,
            tiled=True,
        ),
    )
    flat_query = group_query.reshape(group_size * H_IDX, D_IDX)
    head_weights = group_weight.reshape(group_size, H_IDX).astype(jnp.float32)
    block_width = min(512, ctx_dev)

    def score_block(step, table):
        key_block = lax.dynamic_slice_in_dim(idx_keys, step * block_width, block_width, 0)
        head_dots = lax.dot_general(
            flat_query, key_block, (((1,), (1,)), ((), ())), preferred_element_type=jnp.float32
        )
        active = jnp.maximum(head_dots, 0.0).reshape(group_size, H_IDX, block_width)
        summed = jnp.sum(active * head_weights[:, :, None], axis=1)
        return lax.dynamic_update_slice_in_dim(table, summed, step * block_width, 1)

    scores = lax.fori_loop(
        0, ctx_dev // block_width, score_block, jnp.zeros((group_size, ctx_dev), jnp.float32)
    )
    log_length = jnp.log(jnp.float32(ctx_dev * shard_count))
    score_table = lax.all_to_all(
        scores.astype(jnp.bfloat16), "ctx", split_axis=0, concat_axis=1, tiled=True
    ).astype(scores.dtype)
    row_max = jnp.max(score_table, axis=1, keepdims=True)
    row_total = jnp.sum(jnp.exp(score_table - row_max), axis=1, keepdims=True)
    index_logp = score_table - (row_max + jnp.log(row_total)) + log_length
    group_ids = lax.all_gather(page_ids, "ctx", axis=0, tiled=True)
    owner_shard, slot_rank = slot_ranks(group_ids, pages_dev)
    local_page = group_ids % pages_dev
    chosen = (owner_shard == ctx_index)[:, None, :] & (
        slot_rank[:, None, :] == jnp.arange(capacity)[None, :, None]
    )
    slot_page = jnp.sum(jnp.where(chosen, local_page[:, None, :], 0), axis=2)
    page_store = latent_cache.reshape(pages_dev, PAGE, latent_width)
    slot_keys = page_store[slot_page]
    logit_scale = (QK_NOPE + D_ROPE) ** (-0.5)
    arrived = lax.all_to_all(slot_keys, "ctx", split_axis=0, concat_axis=0, tiled=True)
    own_owner, own_rank = slot_ranks(page_ids.reshape(rows_dev * TOPP), pages_dev)
    slot_index = own_owner * capacity + own_rank
    key_rows = arrived.reshape(shard_count * capacity, PAGE, latent_width)[slot_index]
    key_rows = key_rows.reshape(rows_dev, TOPP * PAGE, latent_width)
    query_rows = q_latent.reshape(rows_dev, H, latent_width)
    logits = (
        jnp.einsum("qhd,qkd->qhk", query_rows, key_rows, preferred_element_type=jnp.float32)
        * logit_scale
    )
    logit_max = jnp.max(logits, axis=2, keepdims=True)
    expo = jnp.exp(logits - logit_max)
    att_weights = (expo / jnp.sum(expo, axis=2, keepdims=True)).astype(jnp.bfloat16)
    mixed_rows = jnp.einsum(
        "qhk,qkd->qhd", att_weights, key_rows[:, :, :D_LAT], preferred_element_type=jnp.float32
    )
    latent_out = mixed_rows.astype(jnp.bfloat16).reshape(rows_dev, H * D_LAT)
    return (index_logp, latent_out)


def solution(mesh):
    in_specs = (
        P("ctx", "qry"),
        P("ctx", "qry"),
        P("ctx", None),
        P(("ctx", "qry"), None),
        P("ctx", None),
        P(("ctx", "qry"), None),
    )
    out_specs = (P(("ctx", "qry"), None), P(("ctx", "qry"), None))
    return jax.shard_map(
        per_device, mesh=mesh, in_specs=in_specs, out_specs=out_specs, check_vma=False
    )
```

profile of v0, /device:TPU:0, one launch (start us, length us, event | category | flops | bytes accessed | tf_op | source)
XLA Modules:
  0.0 134.9 jit_solution(11475658209776853552)
XLA Ops:
  0.6 10.6 %all-gather.3 = bf16[8,4,16]{2,1,0:T(4,128)(2,1)S(1)} all-gather(bf16[1,4,16]{2,1,0:T(4,128)(2,1)} %bitcast.83), channel_id=3, replica_groups=mesh['ctx'=8,'qry'=4] {'ctx'}, dimensions={0}, use_global_device_ids=true | all-gather | bytes 1152 | tf_op jit(solution)/shard_map/all_gather | solution.py:39
  11.2 0.6 copy.20
  11.8 4.9 %all-to-all-start.1 = ((bf16[8,4,1,16]{3,0,2,1:T(8,128)(2,1)}), bf16[8,4,1,16]{3,0,2,1:T(8,128)(2,1)S(1)}, u32[]{:S(2)}, u32[]{:S(2)}) async-start(bf16[8,4,1,16]{3,0,2,1:T(8,128)(2,1)} %copy.20), calls=%async_computation.1 | async-start | bytes 16384 | tf_op jit(solution)/shard_map/all_to_all | solution.py:49
  16.7 8.6 %all-gather.4 = s32[8,1,32]{2,1,0:T(1,128)S(1)} all-gather(s32[1,1,32]{2,1,0:T(1,128)} %bitcast.84), channel_id=1, replica_groups=mesh['ctx'=8,'qry'=4] {'ctx'}, dimensions={0}, use_global_device_ids=true | all-gather | bytes 1152 | tf_op jit(solution)/shard_map/all_gather | solution.py:80
  25.3 0.3 convert_reduce_fusion
  25.6 0.2 select_reduce_fusion
  25.8 8.4 %all-gather.2 = bf16[8,4,2048]{2,1,0:T(4,128)(2,1)S(1)} all-gather(bf16[1,4,2048]{2,1,0:T(4,128)(2,1)} %bitcast.82), channel_id=2, replica_groups=mesh['ctx'=8,'qry'=4] {'ctx'}, dimensions={0}, use_global_device_ids=true | all-gather | bytes 147456 | tf_op jit(solution)/shard_map/all_gather | solution.py:38
  34.3 0.7 copy.18
  35.0 5.1 %all-to-all-start = ((bf16[8,4,1,2048]{3,0,2,1:T(8,128)(2,1)}), bf16[8,4,1,2048]{3,0,2,1:T(8,128)(2,1)S(1)}, u32[]{:S(2)}, u32[]{:S(2)}) async-start(bf16[8,4,1,2048]{3,0,2,1:T(8,128)(2,1)} %copy.18), calls=%async_computation | async-start | bytes 262144 | tf_op jit(solution)/shard_map/all_to_all | solution.py:42
  40.2 6.3 %all-to-all-done = bf16[8,4,1,2048]{3,0,2,1:T(8,128)(2,1)S(1)} async-done(((bf16[8,4,1,2048]{3,0,2,1:T(8,128)(2,1)}), bf16[8,4,1,2048]{3,0,2,1:T(8,128)(2,1)S(1)}, u32[]{:S(2)}, u32[]{:S(2)}) %all-to-all-start) | async-done | bytes 131104 | tf_op jit(solution)/shard_map/all_to_all | solution.py:42
  46.7 5.1 %while.13 = (s32[]{:T(128)}, bf16[8,2048]{1,0:T(8,128)(2,1)S(1)}, bf16[2048,128]{1,0:T(8,128)(2,1)}, bf16[512,128]{1,0:T(8,128)(2,1)S(1)}, f32[8,64]{1,0:T(8,128...) while((s32[]{:T(128)}, bf16[8,2048]{1,0:T(8,128)(2,1)S(1)}, bf16[2048,128]{1,0:T(8,128)(2,1)}, ...), condition=%wide.region_2.0_spmd, body=%wide.region_0.0_spmd.sunk | while | flops 67891208 | bytes 288915 | solution.py:70
  46.7 1.2 multiply_reduce_fusion.2
  48.0 1.2 multiply_reduce_fusion.2
  49.3 1.2 multiply_reduce_fusion.2
  50.5 1.2 multiply_reduce_fusion.2
  51.8 0.5 broadcast.203
  52.3 0.7 reduce.11
  53.0 0.6 reshape.309
  53.6 3.3 %all-to-all-start.2 = ((bf16[8,2,1024]{2,1,0:T(2,128)(2,1)}), bf16[8,2,1024]{2,1,0:T(2,128)(2,1)S(1)}, u32[]{:S(2)}, u32[]{:S(2)}) async-start(bf16[8,2,1024]{2,1,0:T(2,128)(2,1)} %reshape.309), calls=%async_computation.2 | async-start | bytes 65536 | tf_op jit(solution)/shard_map/all_to_all | solution.py:74
  57.0 3.1 %copy.23 = bf16[2048,576]{1,0:T(8,128)(2,1)S(1)} copy(bf16[2048,576]{0,1:T(8,128)(2,1)} %param.12) | data formatting | bytes 4718592 | tf_op args[4]
  60.1 3.5 %gather_fusion = bf16[64,64,576]{2,1,0:T(8,128)(2,1)} fusion(bf16[32,64,576]{2,1,0:T(8,128)(2,1)S(1)} %bitcast.71, s32[1024]{0:T(1024)S(1)} %pad_clamp_fusion.1), kind=kCustom, calls=%fused_computation | custom fusion | bytes 9437440 | tf_op jit(solution)/shard_map/gather | solution.py:88
  63.6 4.8 %all-to-all-start.3 = ((bf16[8,8,64,576]{3,2,1,0:T(8,128)(2,1)}), bf16[8,8,64,576]{3,2,1,0:T(8,128)(2,1)}, u32[]{:S(2)}, u32[]{:S(2)}) async-start(bf16[8,8,64,576]{3,2,1,0:T(8,128)(2,1)} %bitcast.72), calls=%async_computation.3 | async-start | bytes 10485760 | tf_op jit(solution)/shard_map/all_to_all | solution.py:90
  68.4 0.9 reduce.10
  69.7 0.7 reduce_max.23
  71.1 0.7 exponential_reduce_fusion
  73.2 0.7 subtract_add_fusion
  73.9 54.8 %all-to-all-done.3 = bf16[8,8,64,576]{3,2,1,0:T(8,128)(2,1)} async-done(((bf16[8,8,64,576]{3,2,1,0:T(8,128)(2,1)}), bf16[8,8,64,576]{3,2,1,0:T(8,128)(2,1)}, u32[]{:S(2)}, u32[]{:S(2)}) %all-to-all-start.3) | async-done | bytes 4718624 | tf_op jit(solution)/shard_map/all_to_all | solution.py:90
  128.7 3.5 %gather_fusion.1 = bf16[32,64,576]{2,1,0:T(8,128)(2,1)S(1)} fusion(bf16[64,64,576]{2,1,0:T(8,128)(2,1)} %bitcast.13, s32[1024]{0:T(1024)S(1)} %pad_clamp_fusion), kind=kCustom, calls=%fused_computation.1 | custom fusion | bytes 4718720 | tf_op jit(solution)/shard_map/gather | solution.py:93
  132.2 0.9 fusion.13
  133.1 0.3 fusion.5
  133.4 0.6 fusion.4
  134.0 0.9 copy.24
  (28 shorter events, 0.9 us)
Async XLA Ops:
  11.8 23.2 %all-to-all-start.1 = ((bf16[8,4,1,16]{3,0,2,1:T(8,128)(2,1)}), bf16[8,4,1,16]{3,0,2,1:T(8,128)(2,1)S(1)}, u32[]{:S(2)}, u32[]{:S(2)}) async-start(bf16[8,4,1,16]{3,0,2,1:T(8,128)(2,1)} %copy.20), calls=%async_computation.1 | async-start | bytes 16384 | tf_op jit(solution)/shard_map/all_to_all | solution.py:49
  35.0 11.5 %all-to-all-start = ((bf16[8,4,1,2048]{3,0,2,1:T(8,128)(2,1)}), bf16[8,4,1,2048]{3,0,2,1:T(8,128)(2,1)S(1)}, u32[]{:S(2)}, u32[]{:S(2)}) async-start(bf16[8,4,1,2048]{3,0,2,1:T(8,128)(2,1)} %copy.18), calls=%async_computation | async-start | bytes 262144 | tf_op jit(solution)/shard_map/all_to_all | solution.py:42
  53.6 10.0 %all-to-all-start.2 = ((bf16[8,2,1024]{2,1,0:T(2,128)(2,1)}), bf16[8,2,1024]{2,1,0:T(2,128)(2,1)S(1)}, u32[]{:S(2)}, u32[]{:S(2)}) async-start(bf16[8,2,1024]{2,1,0:T(2,128)(2,1)} %reshape.309), calls=%async_computation.2 | async-start | bytes 65536 | tf_op jit(solution)/shard_map/all_to_all | solution.py:74
  63.6 4.8 %copy-start = (bf16[1,73728]{1,0:T(2,128)(2,1)S(1)}, bf16[1,73728]{1,0:T(2,128)(2,1)}, u32[]{:S(2)}) copy-start(bf16[1,73728]{1,0:T(2,128)(2,1)} %param.11) | copy-start | bytes 442372
  63.6 5.8 %copy-start.1 = (s32[1,32]{1,0:T(1,128)S(1)}, s32[1,32]{1,0:T(1,128)}, u32[]{:S(2)}) copy-start(s32[1,32]{1,0:T(1,128)} %param.13) | copy-start | bytes 388
  63.6 65.1 %all-to-all-start.3 = ((bf16[8,8,64,576]{3,2,1,0:T(8,128)(2,1)}), bf16[8,8,64,576]{3,2,1,0:T(8,128)(2,1)}, u32[]{:S(2)}, u32[]{:S(2)}) async-start(bf16[8,8,64,576]{3,2,1,0:T(8,128)(2,1)} %bitcast.72), calls=%async_computation.3 | async-start | bytes 10485760 | tf_op jit(solution)/shard_map/all_to_all | solution.py:90
where the time goes:
time: 136 us; the launch traced here: 135 us
  waiting for transfers between devices  61.1 us (45%)
  blocking collectives  27.6 us (20%)
  starting transfers between devices  18.1 us (13%)
  local copies, waits for them, and re-layouts  14.1 us (10%)
  matrix products  6.35 us (5%)
  other arithmetic  4.78 us (4%)
  between operations  2.79 us (2%)
    all_to_all x1, waiting for transfers between devices, per_device(): lax.all_to_all(slot_keys, 'ctx', split_axis=0, concat_axis=0, tiled=True)  54.8 us
    all_gather x1, blocking collectives, per_device(): lax.all_gather(local_weight, 'ctx', axis=0, tiled=True)  10.6 us
    all_gather x1, blocking collectives, per_device(): group_ids = lax.all_gather(page_ids, 'ctx', axis=0, tiled=True)  8.63 us
    all_gather x1, blocking collectives, per_device(): lax.all_gather(local_query, 'ctx', axis=0, tiled=True)  8.42 us
    all_to_all x1, waiting for transfers between devices, per_device(): lax.all_to_all(every_query.reshape(shard_count, group_count, rows_dev, id...  6.25 us
    all_to_all x1, starting transfers between devices, per_device(): lax.all_to_all(every_query.reshape(shard_count, group_count, rows_dev, id...  5.07 us
    dot_general x4, matrix products, score_block(): lax.dot_general(flat_query, key_block, (((1,), (1,)), ((), ())), preferre...  4.91 us
    all_to_all x1, starting transfers between devices, per_device(): lax.all_to_all(every_weight.reshape(shard_count, group_count, rows_dev, i...  4.87 us
  transfers between devices with their start and end apart: 4, of which 2 were waited for; matrix products, arithmetic and copies ran while one was open for 9% of the time, Pallas kernels for 0%

commit v1 on v0

--- a/solution.py
+++ b/solution.py
@@ -87,7 +87,15 @@
     page_store = latent_cache.reshape(pages_dev, PAGE, latent_width)
     slot_keys = page_store[slot_page]
     logit_scale = (QK_NOPE + D_ROPE) ** (-0.5)
-    arrived = lax.all_to_all(slot_keys, "ctx", split_axis=0, concat_axis=0, tiled=True)
+    ways, here = (lax.axis_size("ctx"), lax.axis_index("ctx"))
+    width = slot_keys.shape[0] // ways
+    turned = jnp.roll(slot_keys, -here * width, axis=0)
+    got = [lax.slice_in_dim(turned, 0, width, axis=0)]
+    for far in range(1, ways):
+        sent = lax.slice_in_dim(turned, far * width, (far + 1) * width, axis=0)
+        got.append(lax.ppermute(sent, "ctx", [(d, (d + far) % ways) for d in range(ways)]))
+    line = jnp.concatenate(got[::-1], axis=0)
+    arrived = jnp.roll(line, (here + 1) * got[0].shape[0], axis=0)
     own_owner, own_rank = slot_ranks(page_ids.reshape(rows_dev * TOPP), pages_dev)
     slot_index = own_owner * capacity + own_rank
     key_rows = arrived.reshape(shard_count * capacity, PAGE, latent_width)[slot_index]

time: 136 us -> 174 us (1.28)
  blocking collectives: 27.6 us -> 78 us
  waiting for transfers between devices: 61.1 us -> 25.9 us
  local copies, waits for them, and re-layouts: 14.1 us -> 25.8 us
  other arithmetic: 4.78 us -> 15 us
    all_to_all x1 -> x0, waiting for transfers between devices: 54.8 us -> none  [per_device(): lax.all_to_all(slot_keys, 'ctx', split_axis=0, concat_axis=0, tiled=True)]
    all_gather x1, blocking collectives: 10.6 us -> 59.3 us  [per_device(): lax.all_gather(local_weight, 'ctx', axis=0, tiled=True)]
    ppermute x0 -> x7, waiting for transfers between devices: none -> 17.5 us  [per_device(): lax.ppermute(sent, 'ctx', [(d, (d + far) % ways) for d in range(ways)])]
    concatenate x0 -> x2, other arithmetic: none -> 9.35 us  [the longest x1 4.75 us: per_device(): turned = jnp.roll(slot_keys, -here * width, axis=0)]
    unnamed x8 -> x21, local copies, waits for them, and re-layouts: 4.66 us -> 13 us
    ppermute x0 -> x7, starting transfers between devices: none -> 5.67 us  [per_device(): lax.ppermute(sent, 'ctx', [(d, (d + far) % ways) for d in range(ways)])]
    all_to_all x1 -> x0, starting transfers between devices: 4.78 us -> none  [per_device(): lax.all_to_all(slot_keys, 'ctx', split_axis=0, concat_axis=0, tiled=True)]
    all_to_all x1, waiting for transfers between devices: 0.01 us -> 2.14 us  [per_device(): lax.all_to_all(scores.astype(jnp.bfloat16), 'ctx', split_axis=0, concat_a...]
  transfers between devices with their start and end apart: 4 -> 10, of which waited for: 2 -> 4; matrix products, arithmetic and copies ran while one was open for 9% -> 11% of each run, Pallas kernels for 0% -> 0%
where the time goes in v1:
time: 174 us; the launch traced here: 173 us
  blocking collectives  78 us (45%)
  waiting for transfers between devices  25.9 us (15%)
  local copies, waits for them, and re-layouts  25.8 us (15%)
  starting transfers between devices  19 us (11%)
  other arithmetic  15 us (9%)
  matrix products  6.35 us (4%)
  between operations  2.86 us (2%)
    all_gather x1, blocking collectives, per_device(): lax.all_gather(local_weight, 'ctx', axis=0, tiled=True)  59.3 us
    ppermute x7, waiting for transfers between devices, per_device(): lax.ppermute(sent, 'ctx', [(d, (d + far) % ways) for d in range(ways)])  17.5 us
    unnamed x21, local copies, waits for them, and re-layouts  13 us
    all_gather x1, blocking collectives, per_device(): group_ids = lax.all_gather(page_ids, 'ctx', axis=0, tiled=True)  10.4 us
    all_gather x1, blocking collectives, per_device(): lax.all_gather(local_query, 'ctx', axis=0, tiled=True)  8.25 us
    all_to_all x1, waiting for transfers between devices, per_device(): lax.all_to_all(every_query.reshape(shard_count, group_count, rows_dev, id...  6.32 us
    ppermute x7, starting transfers between devices, per_device(): lax.ppermute(sent, 'ctx', [(d, (d + far) % ways) for d in range(ways)])  5.67 us
    all_to_all x1, starting transfers between devices, per_device(): lax.all_to_all(every_query.reshape(shard_count, group_count, rows_dev, id...  5.09 us
  transfers between devices with their start and end apart: 10, of which 4 were waited for; matrix products, arithmetic and copies ran while one was open for 11% of the time, Pallas kernels for 0%

profile of v1, /device:TPU:0, one launch (start us, length us, event | category | flops | bytes accessed | tf_op | source)
XLA Modules:
  0.0 173.1 jit_solution(7367100711462379652)
XLA Ops:
  0.7 10.4 %all-gather.4 = s32[8,1,32]{2,1,0:T(1,128)S(1)} all-gather(s32[1,1,32]{2,1,0:T(1,128)} %bitcast.85), channel_id=1, replica_groups=mesh['ctx'=8,'qry'=4] {'ctx'}, dimensions={0}, use_global_device_ids=true | all-gather | bytes 1152 | tf_op jit(solution)/shard_map/all_gather | solution.py:80
  11.7 3.1 %copy.23 = bf16[2048,576]{1,0:T(8,128)(2,1)S(1)} copy(bf16[2048,576]{0,1:T(8,128)(2,1)} %param.14) | data formatting | bytes 4718592 | tf_op args[4]
  14.8 3.5 %gather_fusion = bf16[64,64,576]{2,1,0:T(8,128)(2,1)} fusion(bf16[32,64,576]{2,1,0:T(8,128)(2,1)S(1)} %bitcast.71, s32[1024]{0:T(1024)S(1)} %pad_clamp_fusion.1), kind=kCustom, calls=%fused_computation | custom fusion | bytes 9437440 | tf_op jit(solution)/shard_map/gather | solution.py:88
  18.3 4.8 %fusion.3 = bf16[8,8,64,576]{3,2,1,0:T(8,128)(2,1)S(1)} fusion(s32[]{:T(128)S(6)} %select_n.84, bf16[8,8,64,576]{3,2,1,0:T(8,128)(2,1)} %bitcast.72), kind=kLoop, calls=%fused_computation.12 | loop fusion | flops 2359296 | bytes 9437188 | tf_op jit(solution)/shard_map/jit(_roll_dynamic)/concatenate | solution.py:92
  23.1 2.3 %copy-done = bf16[8,8,64,576]{3,2,1,0:T(8,128)(2,1)} copy-done((bf16[8,8,64,576]{3,2,1,0:T(8,128)(2,1)}, bf16[8,8,64,576]{3,2,1,0:T(8,128)(2,1)S(1)}, u32[]{:S(2)}) %copy-start) | copy-done | bytes 4718616
  25.4 1.5 fusion.15
  26.9 1.3 collective-permute-start
  28.2 1.5 collective-permute-start.1
  30.3 1.5 collective-permute-start.4
  31.8 59.3 %all-gather.3 = bf16[8,4,16]{2,1,0:T(4,128)(2,1)S(1)} all-gather(bf16[1,4,16]{2,1,0:T(4,128)(2,1)S(1)} %bitcast.84), channel_id=3, replica_groups=mesh['ctx'=8,'qry'=4] {'ctx'}, dimensions={0}, use_global_device_ids=true | all-gather | bytes 1152 | tf_op jit(solution)/shard_map/all_gather | solution.py:39
  91.8 4.9 %all-to-all-start.1 = ((bf16[8,4,1,16]{3,0,2,1:T(8,128)(2,1)}), bf16[8,4,1,16]{3,0,2,1:T(8,128)(2,1)S(1)}, u32[]{:S(2)}, u32[]{:S(2)}) async-start(bf16[8,4,1,16]{3,0,2,1:T(8,128)(2,1)} %copy.20), calls=%async_computation.1 | async-start | bytes 16384 | tf_op jit(solution)/shard_map/all_to_all | solution.py:49
  96.8 8.2 %all-gather.2 = bf16[8,4,2048]{2,1,0:T(4,128)(2,1)S(1)} all-gather(bf16[1,4,2048]{2,1,0:T(4,128)(2,1)S(1)} %bitcast.83), channel_id=2, replica_groups=mesh['ctx'=8,'qry'=4] {'ctx'}, dimensions={0}, use_global_device_ids=true | all-gather | bytes 147456 | tf_op jit(solution)/shard_map/all_gather | solution.py:38
  105.8 5.1 %all-to-all-start = ((bf16[8,4,1,2048]{3,0,2,1:T(8,128)(2,1)}), bf16[8,4,1,2048]{3,0,2,1:T(8,128)(2,1)S(1)}, u32[]{:S(2)}, u32[]{:S(2)}) async-start(bf16[8,4,1,2048]{3,0,2,1:T(8,128)(2,1)} %copy.18), calls=%async_computation | async-start | bytes 262144 | tf_op jit(solution)/shard_map/all_to_all | solution.py:42
  111.0 6.3 %all-to-all-done = bf16[8,4,1,2048]{3,0,2,1:T(8,128)(2,1)S(1)} async-done(((bf16[8,4,1,2048]{3,0,2,1:T(8,128)(2,1)}), bf16[8,4,1,2048]{3,0,2,1:T(8,128)(2,1)S(1)}, u32[]{:S(2)}, u32[]{:S(2)}) %all-to-all-start) | async-done | bytes 131104 | tf_op jit(solution)/shard_map/all_to_all | solution.py:42
  117.6 5.1 %while.13 = (s32[]{:T(128)}, bf16[8,2048]{1,0:T(8,128)(2,1)S(1)}, bf16[2048,128]{1,0:T(8,128)(2,1)}, bf16[512,128]{1,0:T(8,128)(2,1)S(1)}, f32[8,64]{1,0:T(8,128...) while((s32[]{:T(128)}, bf16[8,2048]{1,0:T(8,128)(2,1)S(1)}, bf16[2048,128]{1,0:T(8,128)(2,1)}, ...), condition=%wide.region_2.0_spmd, body=%wide.region_0.0_spmd.sunk | while | flops 67891208 | bytes 288915 | solution.py:70
  117.6 1.2 multiply_reduce_fusion.2
  118.8 1.2 multiply_reduce_fusion.2
  120.1 1.2 multiply_reduce_fusion.2
  121.4 1.2 multiply_reduce_fusion.2
  124.4 3.3 %all-to-all-start.2 = ((bf16[8,2,1024]{2,1,0:T(2,128)(2,1)}), bf16[8,2,1024]{2,1,0:T(2,128)(2,1)S(1)}, u32[]{:S(2)}, u32[]{:S(2)}) async-start(bf16[8,2,1024]{2,1,0:T(2,128)(2,1)} %reshape.309), calls=%async_computation.2 | async-start | bytes 65536 | tf_op jit(solution)/shard_map/all_to_all | solution.py:74
  127.8 1.8 %reduce.10 = bf16[73728]{0:T(1024)(128)(2,1)S(1)} reduce(bf16[1,73728]{1,0:T(2,128)(2,1)} %param.13, bf16[]{:T(256)} %constant.119), dimensions={0}, to_apply=%param.13.reduce_sub_computation | reduce | bytes 294914 | tf_op args[3]
  130.4 2.1 %all-to-all-done.2 = bf16[8,2,1024]{2,1,0:T(2,128)(2,1)S(1)} async-done(((bf16[8,2,1024]{2,1,0:T(2,128)(2,1)}), bf16[8,2,1024]{2,1,0:T(2,128)(2,1)S(1)}, u32[]{:S(2)}, u32[]{:S(2)}) %all-to-all-start.2) | async-done | bytes 32800 | tf_op jit(solution)/shard_map/all_to_all | solution.py:74
  137.3 1.1 constant_dynamic-update-slice_fusion.7
  138.7 1.2 constant_dynamic-update-slice_fusion.6
  139.9 1.2 constant_dynamic-update-slice_fusion.5
  141.1 1.2 constant_dynamic-update-slice_fusion.4
  142.3 1.2 constant_dynamic-update-slice_fusion.3
  143.5 11.8 %collective-permute-done.5 = bf16[1,8,64,576]{3,2,1,0:T(8,128)(2,1)S(1)} collective-permute-done((bf16[1,8,64,576]{3,2,1,0:T(8,128)(2,1)S(1)}, bf16[1,8,64,576]{3,2,1,0:T(8,128)(2,1)S(1)}, u32[]{:S(2)}, u32[]{:S(2)}) %collective-permute-start.5) | collective-permute-done | bytes 589856 | tf_op jit(solution)/shard_map/ppermute | solution.py:96
  155.3 5.7 %collective-permute-done.6 = bf16[1,8,64,576]{3,2,1,0:T(8,128)(2,1)S(1)} collective-permute-done((bf16[1,8,64,576]{3,2,1,0:T(8,128)(2,1)S(1)}, bf16[1,8,64,576]{3,2,1,0:T(8,128)(2,1)S(1)}, u32[]{:S(2)}, u32[]{:S(2)}) %collective-permute-start.6) | collective-permute-done | bytes 589856 | tf_op jit(solution)/shard_map/ppermute | solution.py:96
  161.1 1.2 slice_dynamic-update-slice_fusion
  162.3 4.6 %fusion.2 = bf16[8,8,64,576]{3,2,1,0:T(8,128)(2,1)} fusion(s32[]{:T(128)S(6)} %select_n.86, bf16[8,8,64,576]{3,2,1,0:T(8,128)(2,1)S(1)} %slice_dynamic-update-slice_fusion), kind=kLoop, calls=%fused_computation.11 | loop fusion | flops 2359296 | bytes 9437188 | tf_op jit(solution)/shard_map/jit(_roll_dynamic)/concatenate | solution.py:98
  166.9 3.5 %gather_fusion.1 = bf16[32,64,576]{2,1,0:T(8,128)(2,1)S(1)} fusion(bf16[64,64,576]{2,1,0:T(8,128)(2,1)} %bitcast.73, s32[1024]{0:T(1024)S(1)} %pad_clamp_fusion), kind=kCustom, calls=%fused_computation.1 | custom fusion | bytes 4718720 | tf_op jit(solution)/shard_map/gather | solution.py:101
  (57 shorter events, 11.6 us)
Async XLA Ops:
  23.1 2.3 %copy-start = (bf16[8,8,64,576]{3,2,1,0:T(8,128)(2,1)}, bf16[8,8,64,576]{3,2,1,0:T(8,128)(2,1)S(1)}, u32[]{:S(2)}) copy-start(bf16[8,8,64,576]{3,2,1,0:T(8,128)(2,1)S(1)} %fusion.3) | copy-start | bytes 14155780
  25.4 6.4 %copy-start.3 = (bf16[4,16]{1,0:T(4,128)(2,1)S(1)}, bf16[4,16]{1,0:T(4,128)(2,1)}, u32[]{:S(2)}) copy-start(bf16[4,16]{1,0:T(4,128)(2,1)} %param.11) | copy-start | bytes 388
  25.4 71.2 %copy-start.4 = (s32[1,32]{1,0:T(1,128)S(1)}, s32[1,32]{1,0:T(1,128)}, u32[]{:S(2)}) copy-start(s32[1,32]{1,0:T(1,128)} %param.15) | copy-start | bytes 388
  25.4 71.5 %copy-start.2 = (bf16[4,2048]{1,0:T(4,128)(2,1)S(1)}, bf16[4,2048]{1,0:T(4,128)(2,1)}, u32[]{:S(2)}) copy-start(bf16[4,2048]{1,0:T(4,128)(2,1)} %param.10) | copy-start | bytes 49156
  26.9 109.8 %collective-permute-start = (bf16[1,8,64,576]{3,2,1,0:T(8,128)(2,1)}, bf16[1,8,64,576]{3,2,1,0:T(8,128)(2,1)}, u32[]{:S(2)}, u32[]{:S(2)}) collective-permute-start(bf16[1,8,64,576]{3,2,1,0:T(8,128)(2,1)} %get-tuple-element.116), channel_id=1, source_target_pairs={{0,28},{4,0},{8,4},{12,8},{16,12},{20,16},{24,20},{28,24},{1,29},{... | collective-permute-start | bytes 1769480 | tf_op jit(solution)/shard_map/ppermute | solution.py:96
  28.2 110.2 %collective-permute-start.1 = (bf16[1,8,64,576]{3,2,1,0:T(8,128)(2,1)}, bf16[1,8,64,576]{3,2,1,0:T(8,128)(2,1)}, u32[]{:S(2)}, u32[]{:S(2)}) collective-permute-start(bf16[1,8,64,576]{3,2,1,0:T(8,128)(2,1)} %get-tuple-element.115), channel_id=1, source_target_pairs={{0,24},{4,28},{8,0},{12,4},{16,8},{20,12},{24,16},{28,20},{1,25},{... | collective-permute-start | bytes 1769480 | tf_op jit(solution)/shard_map/ppermute | solution.py:96
  29.7 110.1 %collective-permute-start.2 = (bf16[1,8,64,576]{3,2,1,0:T(8,128)(2,1)S(1)}, bf16[1,8,64,576]{3,2,1,0:T(8,128)(2,1)}, u32[]{:S(2)}, u32[]{:S(2)}) collective-permute-start(bf16[1,8,64,576]{3,2,1,0:T(8,128)(2,1)S(1)} %get-tuple-element.114), channel_id=1, source_target_pairs={{0,20},{4,24},{8,28},{12,0},{16,4},{20,8},{24,12},{28,16},{1,21},{... | collective-permute-start | bytes 1769480 | tf_op jit(solution)/shard_map/ppermute | solution.py:96
  29.7 111.3 %collective-permute-start.3 = (bf16[1,8,64,576]{3,2,1,0:T(8,128)(2,1)S(1)}, bf16[1,8,64,576]{3,2,1,0:T(8,128)(2,1)}, u32[]{:S(2)}, u32[]{:S(2)}) collective-permute-start(bf16[1,8,64,576]{3,2,1,0:T(8,128)(2,1)S(1)} %get-tuple-element.113), channel_id=1, source_target_pairs={{0,16},{4,20},{8,24},{12,28},{16,0},{20,4},{24,8},{28,12},{1,17},{... | collective-permute-start | bytes 1769480 | tf_op jit(solution)/shard_map/ppermute | solution.py:96
  30.3 111.9 %collective-permute-start.4 = (bf16[1,8,64,576]{3,2,1,0:T(8,128)(2,1)S(1)}, bf16[1,8,64,576]{3,2,1,0:T(8,128)(2,1)}, u32[]{:S(2)}, u32[]{:S(2)}) collective-permute-start(bf16[1,8,64,576]{3,2,1,0:T(8,128)(2,1)S(1)} %get-tuple-element.112), channel_id=1, source_target_pairs={{0,12},{4,16},{8,20},{12,24},{16,28},{20,0},{24,4},{28,8},{1,13},{... | collective-permute-start | bytes 1769480 | tf_op jit(solution)/shard_map/ppermute | solution.py:96
  91.8 14.1 %all-to-all-start.1 = ((bf16[8,4,1,16]{3,0,2,1:T(8,128)(2,1)}), bf16[8,4,1,16]{3,0,2,1:T(8,128)(2,1)S(1)}, u32[]{:S(2)}, u32[]{:S(2)}) async-start(bf16[8,4,1,16]{3,0,2,1:T(8,128)(2,1)} %copy.20), calls=%async_computation.1 | async-start | bytes 16384 | tf_op jit(solution)/shard_map/all_to_all | solution.py:49
  105.8 11.5 %all-to-all-start = ((bf16[8,4,1,2048]{3,0,2,1:T(8,128)(2,1)}), bf16[8,4,1,2048]{3,0,2,1:T(8,128)(2,1)S(1)}, u32[]{:S(2)}, u32[]{:S(2)}) async-start(bf16[8,4,1,2048]{3,0,2,1:T(8,128)(2,1)} %copy.18), calls=%async_computation | async-start | bytes 262144 | tf_op jit(solution)/shard_map/all_to_all | solution.py:42
  124.4 8.1 %all-to-all-start.2 = ((bf16[8,2,1024]{2,1,0:T(2,128)(2,1)}), bf16[8,2,1024]{2,1,0:T(2,128)(2,1)S(1)}, u32[]{:S(2)}, u32[]{:S(2)}) async-start(bf16[8,2,1024]{2,1,0:T(2,128)(2,1)} %reshape.309), calls=%async_computation.2 | async-start | bytes 65536 | tf_op jit(solution)/shard_map/all_to_all | solution.py:74
  136.7 18.5 %collective-permute-start.5 = (bf16[1,8,64,576]{3,2,1,0:T(8,128)(2,1)S(1)}, bf16[1,8,64,576]{3,2,1,0:T(8,128)(2,1)S(1)}, u32[]{:S(2)}, u32[]{:S(2)}) collective-permute-start(bf16[1,8,64,576]{3,2,1,0:T(8,128)(2,1)S(1)} %get-tuple-element.111), channel_id=1, source_target_pairs={{0,8},{4,12},{8,16},{12,20},{16,24},{20,28},{24,0},{28,4},{1,9},{5... | collective-permute-start | bytes 1769480 | tf_op jit(solution)/shard_map/ppermute | solution.py:96
  138.4 22.6 %collective-permute-start.6 = (bf16[1,8,64,576]{3,2,1,0:T(8,128)(2,1)S(1)}, bf16[1,8,64,576]{3,2,1,0:T(8,128)(2,1)S(1)}, u32[]{:S(2)}, u32[]{:S(2)}) collective-permute-start(bf16[1,8,64,576]{3,2,1,0:T(8,128)(2,1)S(1)} %get-tuple-element.110), channel_id=1, source_target_pairs={{0,4},{4,8},{8,12},{12,16},{16,20},{20,24},{24,28},{28,0},{1,5},{5... | collective-permute-start | bytes 1769480 | tf_op jit(solution)/shard_map/ppermute | solution.py:96
  166.9 3.6 %copy-start.1 = (bf16[128,576]{1,0:T(8,128)(2,1)S(1)}, bf16[128,576]{1,0:T(8,128)(2,1)}, u32[]{:S(2)}) copy-start(bf16[128,576]{1,0:T(8,128)(2,1)} %reshape.274) | copy-start | bytes 442372
